TPU v7x, 256 devices: a whole 4x4x8 slice. The times are simulated.
256 devices in a mesh: row: 8 (over z), col: 32 (over x, y, core).
Axes of the slice: x: 4, y: 4, z: 8, core: 2. Of those that a mesh axis runs over, the one named last changes fastest.
Arguments:
- a_trail: float32 [16384, 16384], P('row', 'col'), may hold values from -60 to 60, as said below
- a_panel: float32 [16384, 256], P(('row', 'col')), may hold values from -6 to 6
- l_panel: float32 [16384, 256], P(('row', 'col')), may hold values from -0.5 to 0.5
- a_diag: float32 [256, 256], replicated, may hold values from -60 to 60, as said below
- l_inverse: float32 [256, 256], replicated, may hold values from -4 to 4, as said below
Outputs:
- trail_out: float32 [16384, 16384], P('row', 'col')
- panel_out: float32 [16384, 256], P(('row', 'col'))
Inputs may be any that keep to these rules, and one draw needn't show every extreme that they name: `a_trail`: symmetric. `a_diag`: symmetric. `l_inverse`: lower triangular with a positive diagonal.
All inputs are finite; a program needn't handle non-finite values.
Results may differ from a plain program's by a relative error of at most 0.0003.
Values sent between devices are 32-bit elements; how exact they have to be, the bound alone decides.
No kernel may reach another device: no remote copies, remote signals or barrier semaphores. Data moves between devices by JAX's collectives and lax.ppermute only.
A program may use at most 64 MiB of HBM per device.

v0:
```python
import jax
import jax.numpy as jnp
from jax import lax
from jax.sharding import PartitionSpec as P

NS_STEPS = 8
ROWS = 8
COLS = 32
BOTH = ("row", "col")


def product(left, right):
    return jnp.dot(left, right, precision=lax.Precision.HIGHEST, preferred_element_type=jnp.float32)


def product3(left, right):
    return jnp.dot(left, right, precision=lax.Precision.HIGH, preferred_element_type=jnp.float32)


def right_solve(factor, values):
    return lax.linalg.triangular_solve(
        factor, values, left_side=False, lower=True, transpose_a=True
    )


def newton_inverse_of_shifted(top):
    size = top.shape[0]
    residual = -top
    approx = jnp.eye(size, dtype=jnp.float32) + residual
    for step in range(1, NS_STEPS):
        residual = product(residual, residual)
        approx = approx + product(approx, residual)
    return approx


def share(block, axis, size):
    parts = lax.all_to_all(jnp.tile(block, (size, 1)), axis, 0, 0, tiled=True)
    return parts.reshape((size,) + block.shape)


def gather_small(block, axis, size):
    return share(block, axis, size).reshape(size * block.shape[0], block.shape[1])


def scatter_sum(block, axis, size):
    parts = lax.all_to_all(block, axis, 0, 0, tiled=True)
    return jnp.sum(parts.reshape(size, block.shape[0] // size, block.shape[1]), axis=0)


def to_columns(block):
    return lax.ppermute(block, BOTH, [(at, at % 8 * COLS + at // 8) for at in range(ROWS * COLS)])


def to_panel(block):
    return lax.ppermute(block, BOTH, [(at % 8 * COLS + at // 8, at) for at in range(ROWS * COLS)])


def scatter_from_first_row(block):
    size = block.shape[0] // ROWS
    total = jnp.where(lax.axis_index("row") == 0, block[:size], 0.0)
    for at in range(1, ROWS):
        total = total + lax.ppermute(block[at * size : (at + 1) * size], "row", [(0, at)])
    return total


def shards(a_trail, a_panel, l_panel, a_diag, l_inverse):
    row_dev, col_dev = a_trail.shape
    nb = a_diag.shape[0]
    part = col_dev // ROWS
    row = lax.axis_index("row")
    col = lax.axis_index("col")
    raw_rows = lax.all_gather(jnp.concatenate([a_panel, l_panel], 1), "col", axis=0, tiled=True)
    a11_new = product(product(l_inverse, a_diag), l_inverse.T)
    half_term = 0.5 * product(l_panel, a11_new)
    first_y = product(a_panel, l_inverse.T) - half_term
    panel_out = first_y - half_term
    mates = gather_small(
        to_columns(jnp.concatenate([product(l_panel, l_inverse), panel_out], 1)), "row", ROWS
    )
    updated = a_trail - product3(raw_rows, mates.T)
    local = lax.iota(jnp.int32, col_dev)
    not_top = jnp.logical_or(col > 0, local >= nb)
    head = updated[: 2 * nb]
    panel_t = jnp.where(not_top[None, :], head[:nb], 0.0)
    shard = scatter_from_first_row(jnp.concatenate([panel_t, head[nb:]], 0).T)
    both_rows = lax.all_gather(to_panel(shard), "col", axis=0, tiled=True)
    panel_rows, second_rows = (both_rows[:, :nb], both_rows[:, nb:])
    corner = jnp.where(col == 0, head[nb:], 0.0)
    packed = scatter_sum(jnp.concatenate([product(panel_t, panel_t.T), corner], 1), "col", COLS)
    packed = gather_small(share(packed, "row", ROWS)[0], "col", COLS)
    gram, top_block, corner = (packed[:, :nb], packed[:, nb : 2 * nb], packed[:, 2 * nb :])
    partial = product3(updated.T, panel_rows)
    image = scatter_sum(partial, "row", ROWS)
    image_rows = lax.all_gather(to_panel(image), "col", axis=0, tiled=True)
    cols = lax.all_gather(jnp.concatenate([shard, image], 1), "row", axis=0, tiled=True)
    panel_cols, second_cols, image_cols = (cols[:, :nb], cols[:, nb : 2 * nb], cols[:, 2 * nb :])
    weights = jnp.concatenate(
        [product(shard[:, :nb].T, image), jnp.where(col == 0, partial[nb : 2 * nb], 0.0)], 1
    )
    weights = scatter_sum(weights, "col", COLS)
    weights = gather_small(jnp.sum(share(weights, "row", ROWS), axis=0), "col", COLS)
    core, image_top = (weights[:, :nb], weights[:, nb:])
    factor = jnp.linalg.cholesky(gram)
    solve = right_solve(factor, jnp.eye(nb, dtype=jnp.float32))
    g_inverse = newton_inverse_of_shifted(product(top_block, solve)).T
    image_top = product(image_top, solve)
    middle = product(product(solve.T, core), solve) + image_top + image_top.T + corner
    m_core = product(g_inverse.T, product(middle, g_inverse))
    solve_g = product(solve, g_inverse)

    def reflectors(panel, image, second, owner):
        size = panel.shape[0]
        picker = jnp.logical_and(
            lax.iota(jnp.int32, size)[:, None] - nb == lax.iota(jnp.int32, nb)[None, :], owner
        ).astype(jnp.float32)
        y_part = product3(panel, solve) + picker
        x_part = product3(image, solve_g) + product3(second, g_inverse)
        return (y_part, x_part - 0.5 * product3(y_part, m_core))

    y_rows, z_rows = reflectors(panel_rows, image_rows, second_rows, row == 0)
    y_cols, z_cols = reflectors(panel_cols, image_cols, second_cols, col == 0)
    trail_out = updated - product3(
        jnp.concatenate([z_rows, y_rows], 1), jnp.concatenate([y_cols, z_cols], 1).T
    )
    return (trail_out, panel_out)


def solution(mesh):
    return jax.shard_map(
        shards,
        mesh=mesh,
        in_specs=(P("row", "col"), P(("row", "col"), None), P(("row", "col"), None), P(), P()),
        out_specs=(P("row", "col"), P(("row", "col"), None)),
        check_vma=False,
    )
```

profile of v0, /device:TPU:1, one launch (start us, length us, event | category | flops | bytes accessed | tf_op | source)
XLA Modules:
  0.0 394.2 jit_solution(14805733286405899376)
XLA Ops:
  12.4 4.9 %collective-permute-start = (f32[64,512]{1,0:T(8,128)S(1)}, f32[64,512]{1,0:T(8,128)S(1)}, u32[]{:S(2)}, u32[]{:S(2)}) collective-permute-start(f32[64,512]{1,0:T(8,128)S(1)} %pad_maximum_fusion.3), channel_id=1, source_target_pairs={{0,0},{1,32},{2,64},{3,96},{4,128},{5,160},{6,192},{7,224},{8,1},{... | collective-permute-start | bytes 393224 | tf_op jit(solution)/shard_map/ppermute | solution.py:51
  20.7 19.2 %all-to-all-start = ((f32[8,64,512]{2,1,0:T(8,128)}), f32[8,64,512]{2,1,0:T(8,128)S(1)}, u32[]{:S(2)}, u32[]{:S(2)}) async-start(f32[8,64,512]{2,1,0:T(8,128)} %tile.12), calls=%async_computation | async-start | bytes 2097152 | tf_op jit(solution)/shard_map/all_to_all | solution.py:37
  40.0 29.2 %all-to-all-done = f32[8,64,512]{2,1,0:T(8,128)S(1)} async-done(((f32[8,64,512]{2,1,0:T(8,128)}), f32[8,64,512]{2,1,0:T(8,128)S(1)}, u32[]{:S(2)}, u32[]{:S(2)}) %all-to-all-start) | async-done | bytes 1048608 | tf_op jit(solution)/shard_map/all_to_all | solution.py:37
  69.1 8.1 %convolution_subtract_fusion = f32[2048,512]{1,0:T(8,128)S(1)} fusion(f32[2048,512]{1,0:T(8,128)} %param.5, f32[2048,512]{1,0:T(8,128)} %all-gather.5.cloned.1.call-done, f32[512,512]{1,0:T(8,128)S(1)} %bitcast.109), kind=kOutput, calls=%fused_computation.7 | convolution fusion | flops 3222274048 | bytes 13631488 | tf_op jit(solution)/shard_map/dot_general | solution.py:17
  98.9 5.5 %collective-permute-done.4 = f32[64,512]{0,1:T(8,128)} collective-permute-done((f32[64,512]{0,1:T(8,128)S(1)}, f32[64,512]{0,1:T(8,128)}, u32[]{:S(2)}, u32[]{:S(2)}) %collective-permute-start.4) | collective-permute-done | bytes 131104 | tf_op jit(solution)/shard_map/ppermute | solution.py:62
  113.3 22.2 %collective-permute-done.8 = f32[64,512]{0,1:T(8,128)S(1)} collective-permute-done((f32[64,512]{0,1:T(8,128)S(1)}, f32[64,512]{0,1:T(8,128)S(1)}, u32[]{:S(2)}, u32[]{:S(2)}) %collective-permute-start.8) | collective-permute-done | bytes 131104 | tf_op jit(solution)/shard_map/ppermute | solution.py:55
  137.0 28.0 %all_to_all.66 = f32[32,8,768]{2,1,0:T(8,128)S(1)} all-to-all(f32[32,8,768]{2,1,0:T(8,128)S(1)} %maximum_bitcast_fusion.1), channel_id=1, replica_groups=mesh['row'=8,'col'=32] {'col'}, dimensions={0} | all-to-all | bytes 1572864 | tf_op jit(solution)/shard_map/all_to_all | solution.py:46
  165.1 14.7 %all_to_all.67 = f32[8,8,768]{2,1,0:T(8,128)S(1)} all-to-all(f32[8,8,768]{2,1,0:T(8,128)S(1)} %tile.13), channel_id=1, replica_groups=mesh['row'=8,'col'=32] {'row'}, dimensions={0} | all-to-all | bytes 393216 | tf_op jit(solution)/shard_map/all_to_all | solution.py:37
  180.7 4.6 %all-to-all-start.4 = ((f32[32,8,768]{2,1,0:T(8,128)}), f32[32,8,768]{2,1,0:T(8,128)S(1)}, u32[]{:S(2)}, u32[]{:S(2)}) async-start(f32[32,8,768]{2,1,0:T(8,128)} %tile.15), calls=%async_computation.4 | async-start | bytes 1572864 | tf_op jit(solution)/shard_map/all_to_all | solution.py:37
  185.4 14.1 %all-to-all-done.4 = f32[32,8,768]{2,1,0:T(8,128)S(1)} async-done(((f32[32,8,768]{2,1,0:T(8,128)}), f32[32,8,768]{2,1,0:T(8,128)S(1)}, u32[]{:S(2)}, u32[]{:S(2)}) %all-to-all-start.4) | async-done | bytes 786464 | tf_op jit(solution)/shard_map/all_to_all | solution.py:37
  199.7 11.7 %cholesky.50 = f32[128,128]{1,0:T(8,128)S(1)} custom-call(f32[128,128]{1,0:T(8,128)S(1)} %cholesky.118), custom_call_target="Cholesky" | custom-call | tf_op jit(solution)/shard_map/jit(cholesky)/cholesky | solution.py:103
  211.5 9.8 %custom-call.14 = f32[1,128,128]{1,2,0:T(8,128)S(1)} custom-call(f32[1,128,128]{2,1,0:T(8,128)S(1)} %get-tuple-element.33), custom_call_target="InvertDiagBlocksLowerTriangular" | custom-call | tf_op jit(solution)/shard_map/jit(cholesky)/cholesky | solution.py:103
  221.8 11.7 %cholesky.105 = f32[128,128]{1,0:T(8,128)S(1)} custom-call(f32[128,128]{1,0:T(8,128)S(1)} %convolution_subtract_fusion.2), custom_call_target="Cholesky" | custom-call | tf_op jit(solution)/shard_map/jit(cholesky)/cholesky | solution.py:103
  239.3 19.8 %custom-call.15 = f32[2,128,128]{1,2,0:T(8,128)S(1)} custom-call(f32[2,128,128]{2,1,0:T(8,128)S(1)} %get-tuple-element.9), custom_call_target="InvertDiagBlocksLowerTriangular" | custom-call | tf_op jit(solution)/shard_map/triangular_solve | solution.py:21
  259.9 7.1 %fusion.12 = f32[512,256]{1,0:T(8,128)} fusion(f32[2048,512]{1,0:T(8,128)} %copy-done.1, f32[2048,512]{1,0:T(8,128)} %all-gather.7.cloned.1.call-done), kind=kOutput, calls=%fused_computation.17 | convolution fusion | flops 1610612736 | bytes 6815744 | tf_op jit(solution)/shard_map/dot_general | solution.py:17
  267.0 5.2 %all-to-all-start.1 = ((f32[8,64,256]{2,1,0:T(8,128)}), f32[8,64,256]{2,1,0:T(8,128)S(1)}, u32[]{:S(2)}, u32[]{:S(2)}) async-start(f32[8,64,256]{2,1,0:T(8,128)} %bitcast.3), calls=%async_computation.1 | async-start | bytes 1048576 | tf_op jit(solution)/shard_map/all_to_all | solution.py:46
  273.8 16.4 %all-to-all-done.1 = f32[8,64,256]{2,1,0:T(8,128)S(1)} async-done(((f32[8,64,256]{2,1,0:T(8,128)}), f32[8,64,256]{2,1,0:T(8,128)S(1)}, u32[]{:S(2)}, u32[]{:S(2)}) %all-to-all-start.1) | async-done | bytes 524320 | tf_op jit(solution)/shard_map/all_to_all | solution.py:46
  299.5 7.1 %all-to-all-start.5 = ((f32[32,8,512]{2,1,0:T(8,128)}), f32[32,8,512]{2,1,0:T(8,128)S(1)}, u32[]{:S(2)}, u32[]{:S(2)}) async-start(f32[32,8,512]{2,1,0:T(8,128)} %maximum_bitcast_fusion.2), calls=%async_computation.5 | async-start | bytes 1048576 | tf_op jit(solution)/shard_map/all_to_all | solution.py:46
  308.7 9.5 %all-to-all-done.5 = f32[32,8,512]{2,1,0:T(8,128)S(1)} async-done(((f32[32,8,512]{2,1,0:T(8,128)}), f32[32,8,512]{2,1,0:T(8,128)S(1)}, u32[]{:S(2)}, u32[]{:S(2)}) %all-to-all-start.5) | async-done | bytes 524320 | tf_op jit(solution)/shard_map/all_to_all | solution.py:46
  319.0 4.9 %all-to-all-start.6 = ((f32[8,8,512]{2,1,0:T(8,128)}), f32[8,8,512]{2,1,0:T(8,128)S(1)}, u32[]{:S(2)}, u32[]{:S(2)}) async-start(f32[8,8,512]{2,1,0:T(8,128)} %tile.16), calls=%async_computation.6 | async-start | bytes 262144 | tf_op jit(solution)/shard_map/all_to_all | solution.py:37
  325.1 8.0 %all-to-all-done.6 = f32[8,8,512]{2,1,0:T(8,128)S(1)} async-done(((f32[8,8,512]{2,1,0:T(8,128)}), f32[8,8,512]{2,1,0:T(8,128)S(1)}, u32[]{:S(2)}, u32[]{:S(2)}) %all-to-all-start.6) | async-done | bytes 131104 | tf_op jit(solution)/shard_map/all_to_all | solution.py:37
  343.7 6.7 %all-to-all-done.7 = f32[32,8,512]{2,1,0:T(8,128)S(1)} async-done(((f32[32,8,512]{2,1,0:T(8,128)}), f32[32,8,512]{2,1,0:T(8,128)S(1)}, u32[]{:S(2)}, u32[]{:S(2)}) %all-to-all-start.7) | async-done | bytes 524320 | tf_op jit(solution)/shard_map/all_to_all | solution.py:37
  365.2 12.7 %all-gather.9.cloned.1.call-done = f32[2048,256]{1,0:T(8,128)} async-done(((f32[64,256]{1,0:T(8,128)}), f32[2048,256]{1,0:T(8,128)}) %all-gather.9.cloned.1.call-update) | async-done | bytes 2097168 | tf_op jit(solution)/shard_map/all_gather | solution.py:94
  382.2 5.2 %fusion.4 = f32[2048,512]{1,0:T(8,128)} fusion(f32[2048,512]{1,0:T(8,128)S(1)} %copy-done.2, f32[2048,256]{0,1:T(8,128)S(1)} %convolution_add_fusion, f32[2048,256]{0,1:T(8,128)S(1)} %fusion.7, f32[512,256]{0,1:T(8,128)S(1)} %copy-done.9, f32[512,256]{0,1:T(8,128)S(1)} %convolution_add_fusion.3), kind=kOutput, calls=%fused_computation.6 | convolution fusion | flops 3223584768 | bytes 13631488 | tf_op jit(solution)/shard_map/dot_general | solution.py:17
  (150 shorter events, 95.5 us)
Async XLA Ops:
  7.2 4.8 %copy-start.13 = (f32[64,256]{1,0:T(8,128)S(1)}, f32[64,256]{1,0:T(8,128)}, u32[]{:S(2)}) copy-start(f32[64,256]{1,0:T(8,128)} %param.6) | copy-start | bytes 196612
  7.2 61.9 %all-gather.5.cloned.1.call-start = ((), (), s32[]{:S(2)}) async-start(), calls=%async_computation.8 | async-start | bytes 4325376 | tf_op jit(solution)/shard_map/all_gather | solution.py:72
  12.4 64.9 %copy-start.14 = (f32[64,256]{1,0:T(8,128)}, f32[64,256]{1,0:T(8,128)S(1)}, u32[]{:S(2)}) copy-start(f32[64,256]{1,0:T(8,128)S(1)} %fusion.18) | copy-start | bytes 196612
  12.4 7.2 %collective-permute-start = (f32[64,512]{1,0:T(8,128)S(1)}, f32[64,512]{1,0:T(8,128)S(1)}, u32[]{:S(2)}, u32[]{:S(2)}) collective-permute-start(f32[64,512]{1,0:T(8,128)S(1)} %pad_maximum_fusion.3), channel_id=1, source_target_pairs={{0,0},{1,32},{2,64},{3,96},{4,128},{5,160},{6,192},{7,224},{8,1},{... | collective-permute-start | bytes 393224 | tf_op jit(solution)/shard_map/ppermute | solution.py:51
  20.7 48.5 %all-to-all-start = ((f32[8,64,512]{2,1,0:T(8,128)}), f32[8,64,512]{2,1,0:T(8,128)S(1)}, u32[]{:S(2)}, u32[]{:S(2)}) async-start(f32[8,64,512]{2,1,0:T(8,128)} %tile.12), calls=%async_computation | async-start | bytes 2097152 | tf_op jit(solution)/shard_map/all_to_all | solution.py:37
  39.9 219.9 %all-gather.7.cloned.1.call-start = ((), (), s32[]{:S(2)}) async-start(), calls=%async_computation.9 | async-start | bytes 4325376 | tf_op jit(solution)/shard_map/all_gather | solution.py:86
  80.3 11.7 %collective-permute-start.1 = (f32[64,512]{0,1:T(8,128)S(1)}, f32[64,512]{0,1:T(8,128)S(1)}, u32[]{:S(2)}, u32[]{:S(2)}) collective-permute-start(f32[64,512]{0,1:T(8,128)S(1)} %get-tuple-element.23), channel_id=1, source_target_pairs={{0,32},{1,33},{2,34},{3,35},{4,36},{5,37},{6,38},{7,39},{8,40},{9,... | collective-permute-start | bytes 393224 | tf_op jit(solution)/shard_map/ppermute | solution.py:62
  82.5 11.6 %collective-permute-start.2 = (f32[64,512]{0,1:T(8,128)S(1)}, f32[64,512]{0,1:T(8,128)S(1)}, u32[]{:S(2)}, u32[]{:S(2)}) collective-permute-start(f32[64,512]{0,1:T(8,128)S(1)} %get-tuple-element.29), channel_id=1, source_target_pairs={{0,64},{1,65},{2,66},{3,67},{4,68},{5,69},{6,70},{7,71},{8,72},{9,... | collective-permute-start | bytes 393224 | tf_op jit(solution)/shard_map/ppermute | solution.py:62
  84.1 14.8 %collective-permute-start.3 = (f32[64,512]{0,1:T(8,128)}, f32[64,512]{0,1:T(8,128)}, u32[]{:S(2)}, u32[]{:S(2)}) collective-permute-start(f32[64,512]{0,1:T(8,128)} %get-tuple-element.28), channel_id=1, source_target_pairs={{0,96},{1,97},{2,98},{3,99},{4,100},{5,101},{6,102},{7,103},{8,104... | collective-permute-start | bytes 393224 | tf_op jit(solution)/shard_map/ppermute | solution.py:62
  86.5 17.9 %collective-permute-start.4 = (f32[64,512]{0,1:T(8,128)S(1)}, f32[64,512]{0,1:T(8,128)}, u32[]{:S(2)}, u32[]{:S(2)}) collective-permute-start(f32[64,512]{0,1:T(8,128)S(1)} %get-tuple-element.27), channel_id=1, source_target_pairs={{0,128},{1,129},{2,130},{3,131},{4,132},{5,133},{6,134},{7,135},{8... | collective-permute-start | bytes 393224 | tf_op jit(solution)/shard_map/ppermute | solution.py:62
  90.0 14.4 %collective-permute-start.5 = (f32[64,512]{0,1:T(8,128)S(1)}, f32[64,512]{0,1:T(8,128)}, u32[]{:S(2)}, u32[]{:S(2)}) collective-permute-start(f32[64,512]{0,1:T(8,128)S(1)} %get-tuple-element.26), channel_id=1, source_target_pairs={{0,160},{1,161},{2,162},{3,163},{4,164},{5,165},{6,166},{7,167},{8... | collective-permute-start | bytes 393224 | tf_op jit(solution)/shard_map/ppermute | solution.py:62
  92.0 12.4 %collective-permute-start.6 = (f32[64,512]{0,1:T(8,128)S(1)}, f32[64,512]{0,1:T(8,128)}, u32[]{:S(2)}, u32[]{:S(2)}) collective-permute-start(f32[64,512]{0,1:T(8,128)S(1)} %get-tuple-element.25), channel_id=1, source_target_pairs={{0,192},{1,193},{2,194},{3,195},{4,196},{5,197},{6,198},{7,199},{8... | collective-permute-start | bytes 393224 | tf_op jit(solution)/shard_map/ppermute | solution.py:62
  94.8 13.2 %collective-permute-start.7 = (f32[64,512]{0,1:T(8,128)S(1)}, f32[64,512]{0,1:T(8,128)}, u32[]{:S(2)}, u32[]{:S(2)}) collective-permute-start(f32[64,512]{0,1:T(8,128)S(1)} %get-tuple-element.24), channel_id=1, source_target_pairs={{0,224},{1,225},{2,226},{3,227},{4,228},{5,229},{6,230},{7,231},{8... | collective-permute-start | bytes 393224 | tf_op jit(solution)/shard_map/ppermute | solution.py:62
  109.5 26.0 %collective-permute-start.8 = (f32[64,512]{0,1:T(8,128)S(1)}, f32[64,512]{0,1:T(8,128)S(1)}, u32[]{:S(2)}, u32[]{:S(2)}) collective-permute-start(f32[64,512]{0,1:T(8,128)S(1)} %fusion.38), channel_id=1, source_target_pairs={{0,0},{32,1},{64,2},{96,3},{128,4},{160,5},{192,6},{224,7},{1,8},{... | collective-permute-start | bytes 393224 | tf_op jit(solution)/shard_map/ppermute | solution.py:55
  180.7 18.8 %all-to-all-start.4 = ((f32[32,8,768]{2,1,0:T(8,128)}), f32[32,8,768]{2,1,0:T(8,128)S(1)}, u32[]{:S(2)}, u32[]{:S(2)}) async-start(f32[32,8,768]{2,1,0:T(8,128)} %tile.15), calls=%async_computation.4 | async-start | bytes 1572864 | tf_op jit(solution)/shard_map/all_to_all | solution.py:37
  199.5 73.1 %copy-start.4 = (f32[32,8,768]{2,1,0:T(8,128)}, f32[32,8,768]{2,1,0:T(8,128)S(1)}, u32[]{:S(2)}) copy-start(f32[32,8,768]{2,1,0:T(8,128)S(1)} %all-to-all-done.4) | copy-start | bytes 2359300
  267.0 23.2 %all-to-all-start.1 = ((f32[8,64,256]{2,1,0:T(8,128)}), f32[8,64,256]{2,1,0:T(8,128)S(1)}, u32[]{:S(2)}, u32[]{:S(2)}) async-start(f32[8,64,256]{2,1,0:T(8,128)} %bitcast.3), calls=%async_computation.1 | async-start | bytes 1048576 | tf_op jit(solution)/shard_map/all_to_all | solution.py:46
  272.2 87.2 %all-gather.11.cloned.1.call-start = ((), (), s32[]{:S(2)}) async-start(), calls=%async_computation.11 | async-start | bytes 1769472 | tf_op jit(solution)/shard_map/all_gather | solution.py:95
  295.6 11.3 %collective-permute-start.9 = (f32[64,256]{1,0:T(8,128)S(1)}, f32[64,256]{1,0:T(8,128)S(1)}, u32[]{:S(2)}, u32[]{:S(2)}) collective-permute-start(f32[64,256]{1,0:T(8,128)S(1)} %reduce_sum.36), channel_id=1, source_target_pairs={{0,0},{32,1},{64,2},{96,3},{128,4},{160,5},{192,6},{224,7},{1,8},{... | collective-permute-start | bytes 196616 | tf_op jit(solution)/shard_map/ppermute | solution.py:55
  299.5 18.8 %all-to-all-start.5 = ((f32[32,8,512]{2,1,0:T(8,128)}), f32[32,8,512]{2,1,0:T(8,128)S(1)}, u32[]{:S(2)}, u32[]{:S(2)}) async-start(f32[32,8,512]{2,1,0:T(8,128)} %maximum_bitcast_fusion.2), calls=%async_computation.5 | async-start | bytes 1048576 | tf_op jit(solution)/shard_map/all_to_all | solution.py:46
  306.7 71.3 %all-gather.9.cloned.1.call-start = ((), (), s32[]{:S(2)}) async-start(), calls=%async_computation.10 | async-start | bytes 2162688 | tf_op jit(solution)/shard_map/all_gather | solution.py:94
  319.0 14.1 %all-to-all-start.6 = ((f32[8,8,512]{2,1,0:T(8,128)}), f32[8,8,512]{2,1,0:T(8,128)S(1)}, u32[]{:S(2)}, u32[]{:S(2)}) async-start(f32[8,8,512]{2,1,0:T(8,128)} %tile.16), calls=%async_computation.6 | async-start | bytes 262144 | tf_op jit(solution)/shard_map/all_to_all | solution.py:37
  334.0 16.4 %all-to-all-start.7 = ((f32[32,8,512]{2,1,0:T(8,128)}), f32[32,8,512]{2,1,0:T(8,128)S(1)}, u32[]{:S(2)}, u32[]{:S(2)}) async-start(f32[32,8,512]{2,1,0:T(8,128)} %tile.17), calls=%async_computation.7 | async-start | bytes 1048576 | tf_op jit(solution)/shard_map/all_to_all | solution.py:37
  362.5 15.5 %copy-start.5 = (f32[256,256]{1,0:T(8,128)S(1)}, f32[256,256]{1,0:T(8,128)}, u32[]{:S(2)}) copy-start(f32[256,256]{1,0:T(8,128)} %fusion.54) | copy-start | bytes 786436
  (12 other events, 29.2 us)
Sparse Core Ops, SparseCore 0:
  10.6 57.4 all-gather.4
  136.4 56.2 all-gather.6
  291.3 32.7 all-gather.10
  326.5 51.3 all-gather.8
where the time goes:
time: 401 us; the launch traced here: 394 us
  waiting for transfers between devices  132 us (33%)
  starting transfers between devices  72.6 us (18%)
  other arithmetic  59.5 us (15%)
  matrix products  56.1 us (14%)
  blocking collectives  42.7 us (11%)
  between operations  15.9 us (4%)
  local copies, waits for them, and re-layouts  15 us (4%)
    all_to_all x4, waiting for transfers between devices, share(): parts = lax.all_to_all(jnp.tile(block, (size, 1)), axis, 0, 0, tiled=True)  58 us
    dot_general x11, matrix products, product3(): jnp.dot(left, right, precision=lax.Precision.HIGH, preferred_element_type...  38.3 us
    another operation x6, other arithmetic, shards(): factor = jnp.linalg.cholesky(gram)  34 us
    all_to_all x4, starting transfers between devices, share(): parts = lax.all_to_all(jnp.tile(block, (size, 1)), axis, 0, 0, tiled=True)  32.9 us
    all_to_all x1, blocking collectives, scatter_sum(): parts = lax.all_to_all(block, axis, 0, 0, tiled=True)  28 us
    all_to_all x2, waiting for transfers between devices, scatter_sum(): parts = lax.all_to_all(block, axis, 0, 0, tiled=True)  25.9 us
    ppermute x2, waiting for transfers between devices, to_panel(): lax.ppermute(block, BOTH, [(at % 8 * COLS + at // 8, at) for at in range(...  22.2 us
    another operation x3, other arithmetic, right_solve(): lax.linalg.triangular_solve(factor, values, left_side=False, lower=True,...  19.9 us
  transfers between devices with their start and end apart: 20, of which 12 were waited for; matrix products, arithmetic and copies ran while one was open for 24% of the time, Pallas kernels for 0%

commit v1 on v0

--- a/solution.py
+++ b/solution.py
@@ -7,6 +7,13 @@
 ROWS = 8
 COLS = 32
 BOTH = ("row", "col")
+
+
+def swapped_in(shard, name, along):
+    size = lax.axis_size(name)
+    blocks = jnp.stack([shard for _ in range(size)])
+    blocks = lax.all_to_all(blocks, name, split_axis=0, concat_axis=0)
+    return jnp.concatenate(blocks, axis=along)
 
 
 def product(left, right):
@@ -91,7 +98,7 @@
     gram, top_block, corner = (packed[:, :nb], packed[:, nb : 2 * nb], packed[:, 2 * nb :])
     partial = product3(updated.T, panel_rows)
     image = scatter_sum(partial, "row", ROWS)
-    image_rows = lax.all_gather(to_panel(image), "col", axis=0, tiled=True)
+    image_rows = swapped_in(to_panel(image), "col", 0)
     cols = lax.all_gather(jnp.concatenate([shard, image], 1), "row", axis=0, tiled=True)
     panel_cols, second_cols, image_cols = (cols[:, :nb], cols[:, nb : 2 * nb], cols[:, 2 * nb :])
     weights = jnp.concatenate(

time: 401 us -> 414 us (1.032)
  starting transfers between devices: 72.6 us -> 81.1 us
  waiting for transfers between devices: 132 us -> 139 us
    all_to_all x0 -> x1, waiting for transfers between devices: none -> 15.7 us  [swapped_in(): blocks = lax.all_to_all(blocks, name, split_axis=0, concat_axis=0)]
    all_gather x1 -> x0, waiting for transfers between devices: 12.7 us -> none  [shards(): image_rows = lax.all_gather(to_panel(image), 'col', axis=0, tiled=True)]
    all_to_all x0 -> x1, starting transfers between devices: none -> 11.9 us  [swapped_in(): blocks = lax.all_to_all(blocks, name, split_axis=0, concat_axis=0)]
  transfers between devices with their start and end apart: 20 -> 20, of which waited for: 12 -> 14; matrix products, arithmetic and copies ran while one was open for 24% -> 23% of each run, Pallas kernels for 0% -> 0%
where the time goes in v1:
time: 414 us; the launch traced here: 407 us
  waiting for transfers between devices  139 us (34%)
  starting transfers between devices  81.1 us (20%)
  other arithmetic  59.4 us (14%)
  matrix products  54.9 us (13%)
  blocking collectives  41.4 us (10%)
  between operations  15.8 us (4%)
  local copies, waits for them, and re-layouts  15.1 us (4%)
    all_to_all x4, waiting for transfers between devices, share(): parts = lax.all_to_all(jnp.tile(block, (size, 1)), axis, 0, 0, tiled=True)  56.3 us
    dot_general x11, matrix products, product3(): jnp.dot(left, right, precision=lax.Precision.HIGH, preferred_element_type...  38.7 us
    another operation x6, other arithmetic, shards(): factor = jnp.linalg.cholesky(gram)  33.9 us
    all_to_all x4, starting transfers between devices, share(): parts = lax.all_to_all(jnp.tile(block, (size, 1)), axis, 0, 0, tiled=True)  31.3 us
    all_to_all x1, blocking collectives, scatter_sum(): parts = lax.all_to_all(block, axis, 0, 0, tiled=True)  27.2 us
    all_to_all x2, waiting for transfers between devices, scatter_sum(): parts = lax.all_to_all(block, axis, 0, 0, tiled=True)  26.3 us
    ppermute x2, waiting for transfers between devices, to_panel(): lax.ppermute(block, BOTH, [(at % 8 * COLS + at // 8, at) for at in range(...  24 us
    another operation x3, other arithmetic, right_solve(): lax.linalg.triangular_solve(factor, values, left_side=False, lower=True,...  19.9 us
  transfers between devices with their start and end apart: 20, of which 14 were waited for; matrix products, arithmetic and copies ran while one was open for 23% of the time, Pallas kernels for 0%

profile of v1, /device:TPU:1, one launch (start us, length us, event | category | flops | bytes accessed | tf_op | source)
XLA Modules:
  0.0 407.1 jit_solution(16712418254815661263)
XLA Ops:
  12.4 4.9 %collective-permute-start = (f32[64,512]{1,0:T(8,128)S(1)}, f32[64,512]{1,0:T(8,128)S(1)}, u32[]{:S(2)}, u32[]{:S(2)}) collective-permute-start(f32[64,512]{1,0:T(8,128)S(1)} %pad_maximum_fusion.3), channel_id=1, source_target_pairs={{0,0},{1,32},{2,64},{3,96},{4,128},{5,160},{6,192},{7,224},{8,1},{... | collective-permute-start | bytes 393224 | tf_op jit(solution)/shard_map/ppermute | solution.py:58
  20.7 19.2 %all-to-all-start = ((f32[8,64,512]{2,1,0:T(8,128)}), f32[8,64,512]{2,1,0:T(8,128)S(1)}, u32[]{:S(2)}, u32[]{:S(2)}) async-start(f32[8,64,512]{2,1,0:T(8,128)} %tile.12), calls=%async_computation | async-start | bytes 2097152 | tf_op jit(solution)/shard_map/all_to_all | solution.py:44
  40.0 29.2 %all-to-all-done = f32[8,64,512]{2,1,0:T(8,128)S(1)} async-done(((f32[8,64,512]{2,1,0:T(8,128)}), f32[8,64,512]{2,1,0:T(8,128)S(1)}, u32[]{:S(2)}, u32[]{:S(2)}) %all-to-all-start) | async-done | bytes 1048608 | tf_op jit(solution)/shard_map/all_to_all | solution.py:44
  69.2 8.1 %convolution_subtract_fusion = f32[2048,512]{1,0:T(8,128)S(1)} fusion(f32[2048,512]{1,0:T(8,128)} %param.5, f32[2048,512]{1,0:T(8,128)} %all-gather.4.cloned.1.call-done, f32[512,512]{1,0:T(8,128)S(1)} %bitcast.110), kind=kOutput, calls=%fused_computation.7 | convolution fusion | flops 3222274048 | bytes 13631488 | tf_op jit(solution)/shard_map/dot_general | solution.py:24
  101.1 5.0 %collective-permute-done.2 = f32[64,512]{0,1:T(8,128)} collective-permute-done((f32[64,512]{0,1:T(8,128)S(1)}, f32[64,512]{0,1:T(8,128)}, u32[]{:S(2)}, u32[]{:S(2)}) %collective-permute-start.2) | collective-permute-done | bytes 131104 | tf_op jit(solution)/shard_map/ppermute | solution.py:69
  106.1 5.6 %collective-permute-done.1 = f32[64,512]{0,1:T(8,128)} collective-permute-done((f32[64,512]{0,1:T(8,128)S(1)}, f32[64,512]{0,1:T(8,128)}, u32[]{:S(2)}, u32[]{:S(2)}) %collective-permute-start.1) | collective-permute-done | bytes 131104 | tf_op jit(solution)/shard_map/ppermute | solution.py:69
  117.0 21.8 %collective-permute-done.8 = f32[64,512]{0,1:T(8,128)S(1)} collective-permute-done((f32[64,512]{0,1:T(8,128)S(1)}, f32[64,512]{0,1:T(8,128)S(1)}, u32[]{:S(2)}, u32[]{:S(2)}) %collective-permute-start.8) | collective-permute-done | bytes 131104 | tf_op jit(solution)/shard_map/ppermute | solution.py:62
  140.3 27.2 %all_to_all.71 = f32[32,8,768]{2,1,0:T(8,128)S(1)} all-to-all(f32[32,8,768]{2,1,0:T(8,128)S(1)} %maximum_bitcast_fusion.1), channel_id=1, replica_groups=mesh['row'=8,'col'=32] {'col'}, dimensions={0} | all-to-all | bytes 1572864 | tf_op jit(solution)/shard_map/all_to_all | solution.py:53
  167.6 14.2 %all_to_all.72 = f32[8,8,768]{2,1,0:T(8,128)S(1)} all-to-all(f32[8,8,768]{2,1,0:T(8,128)S(1)} %tile.13), channel_id=1, replica_groups=mesh['row'=8,'col'=32] {'row'}, dimensions={0} | all-to-all | bytes 393216 | tf_op jit(solution)/shard_map/all_to_all | solution.py:44
  187.4 14.1 %all-to-all-done.5 = f32[32,8,768]{2,1,0:T(8,128)S(1)} async-done(((f32[32,8,768]{2,1,0:T(8,128)}), f32[32,8,768]{2,1,0:T(8,128)S(1)}, u32[]{:S(2)}, u32[]{:S(2)}) %all-to-all-start.5) | async-done | bytes 786464 | tf_op jit(solution)/shard_map/all_to_all | solution.py:44
  201.7 11.7 %cholesky.50 = f32[128,128]{1,0:T(8,128)S(1)} custom-call(f32[128,128]{1,0:T(8,128)S(1)} %cholesky.118), custom_call_target="Cholesky" | custom-call | tf_op jit(solution)/shard_map/jit(cholesky)/cholesky | solution.py:110
  213.5 9.8 %custom-call.14 = f32[1,128,128]{1,2,0:T(8,128)S(1)} custom-call(f32[1,128,128]{2,1,0:T(8,128)S(1)} %get-tuple-element.33), custom_call_target="InvertDiagBlocksLowerTriangular" | custom-call | tf_op jit(solution)/shard_map/jit(cholesky)/cholesky | solution.py:110
  223.8 11.7 %cholesky.105 = f32[128,128]{1,0:T(8,128)S(1)} custom-call(f32[128,128]{1,0:T(8,128)S(1)} %convolution_subtract_fusion.2), custom_call_target="Cholesky" | custom-call | tf_op jit(solution)/shard_map/jit(cholesky)/cholesky | solution.py:110
  241.0 19.8 %custom-call.15 = f32[2,128,128]{1,2,0:T(8,128)S(1)} custom-call(f32[2,128,128]{2,1,0:T(8,128)S(1)} %get-tuple-element.9), custom_call_target="InvertDiagBlocksLowerTriangular" | custom-call | tf_op jit(solution)/shard_map/triangular_solve | solution.py:28
  264.6 7.1 %fusion.12 = f32[512,256]{1,0:T(8,128)} fusion(f32[2048,512]{1,0:T(8,128)} %copy-done.1, f32[2048,512]{1,0:T(8,128)} %all-gather.6.cloned.1.call-done), kind=kOutput, calls=%fused_computation.17 | convolution fusion | flops 1610612736 | bytes 6815744 | tf_op jit(solution)/shard_map/dot_general | solution.py:24
  271.8 4.7 %all-to-all-start.1 = ((f32[8,64,256]{2,1,0:T(8,128)}), f32[8,64,256]{2,1,0:T(8,128)S(1)}, u32[]{:S(2)}, u32[]{:S(2)}) async-start(f32[8,64,256]{2,1,0:T(8,128)} %bitcast.3), calls=%async_computation.1 | async-start | bytes 1048576 | tf_op jit(solution)/shard_map/all_to_all | solution.py:53
  278.6 15.8 %all-to-all-done.1 = f32[8,64,256]{2,1,0:T(8,128)S(1)} async-done(((f32[8,64,256]{2,1,0:T(8,128)}), f32[8,64,256]{2,1,0:T(8,128)S(1)}, u32[]{:S(2)}, u32[]{:S(2)}) %all-to-all-start.1) | async-done | bytes 524320 | tf_op jit(solution)/shard_map/all_to_all | solution.py:53
  295.7 5.0 %all-to-all-start.6 = ((f32[32,8,512]{2,1,0:T(8,128)}), f32[32,8,512]{2,1,0:T(8,128)S(1)}, u32[]{:S(2)}, u32[]{:S(2)}) async-start(f32[32,8,512]{2,1,0:T(8,128)} %maximum_bitcast_fusion.2), calls=%async_computation.6 | async-start | bytes 1048576 | tf_op jit(solution)/shard_map/all_to_all | solution.py:53
  301.9 10.5 %all-to-all-done.6 = f32[32,8,512]{2,1,0:T(8,128)S(1)} async-done(((f32[32,8,512]{2,1,0:T(8,128)}), f32[32,8,512]{2,1,0:T(8,128)S(1)}, u32[]{:S(2)}, u32[]{:S(2)}) %all-to-all-start.6) | async-done | bytes 524320 | tf_op jit(solution)/shard_map/all_to_all | solution.py:53
  317.1 9.1 %all-to-all-done.7 = f32[8,8,512]{2,1,0:T(8,128)S(1)} async-done(((f32[8,8,512]{2,1,0:T(8,128)}), f32[8,8,512]{2,1,0:T(8,128)S(1)}, u32[]{:S(2)}, u32[]{:S(2)}) %all-to-all-start.7) | async-done | bytes 131104 | tf_op jit(solution)/shard_map/all_to_all | solution.py:44
  344.4 11.9 %all-to-all-start.2 = ((f32[32,64,256]{2,1,0:T(8,128)}), f32[32,64,256]{2,1,0:T(8,128)}, u32[]{:S(2)}, u32[]{:S(2)}) async-start(f32[32,64,256]{2,1,0:T(8,128)} %stack.2), calls=%async_computation.2 | async-start | bytes 4194304 | tf_op jit(solution)/shard_map/all_to_all | solution.py:15
  368.9 15.7 %all-to-all-done.2 = f32[32,64,256]{2,1,0:T(8,128)} async-done(((f32[32,64,256]{2,1,0:T(8,128)}), f32[32,64,256]{2,1,0:T(8,128)}, u32[]{:S(2)}, u32[]{:S(2)}) %all-to-all-start.2) | async-done | bytes 2097184 | tf_op jit(solution)/shard_map/all_to_all | solution.py:15
  384.6 5.3 %fusion.7 = f32[2048,256]{0,1:T(8,128)} fusion(f32[2048,256]{0,1:T(8,128)} %convolution_multiply_fusion, f32[2048,256]{0,1:T(8,128)} %fusion.8, f32[2048,256]{1,0:T(8,128)} %bitcast.4, f32[256,256]{1,0:T(8,128)S(1)} %fusion.54), kind=kOutput, calls=%fused_computation.11 | convolution fusion | flops 806354944 | bytes 8650752 | tf_op jit(solution)/shard_map/dot_general | solution.py:24
  395.1 5.2 %fusion.4 = f32[2048,512]{1,0:T(8,128)} fusion(f32[2048,512]{1,0:T(8,128)S(1)} %copy-done.2, f32[2048,256]{0,1:T(8,128)S(1)} %convolution_add_fusion, f32[2048,256]{0,1:T(8,128)S(1)} %copy-done.4, f32[512,256]{0,1:T(8,128)S(1)} %fusion.14, f32[512,256]{0,1:T(8,128)S(1)} %convolution_add_fusion.3), kind=kOutput, calls=%fused_computation.6 | convolution fusion | flops 3223584768 | bytes 13631488 | tf_op jit(solution)/shard_map/dot_general | solution.py:24
  (144 shorter events, 102.1 us)
Async XLA Ops:
  7.2 4.8 %copy-start.11 = (f32[64,256]{1,0:T(8,128)S(1)}, f32[64,256]{1,0:T(8,128)}, u32[]{:S(2)}) copy-start(f32[64,256]{1,0:T(8,128)} %param.6) | copy-start | bytes 196612
  7.2 62.0 %all-gather.4.cloned.1.call-start = ((), (), s32[]{:S(2)}) async-start(), calls=%async_computation.9 | async-start | bytes 4325376 | tf_op jit(solution)/shard_map/all_gather | solution.py:79
  12.4 64.9 %copy-start.12 = (f32[64,256]{1,0:T(8,128)}, f32[64,256]{1,0:T(8,128)S(1)}, u32[]{:S(2)}) copy-start(f32[64,256]{1,0:T(8,128)S(1)} %fusion.18) | copy-start | bytes 196612
  12.4 7.2 %collective-permute-start = (f32[64,512]{1,0:T(8,128)S(1)}, f32[64,512]{1,0:T(8,128)S(1)}, u32[]{:S(2)}, u32[]{:S(2)}) collective-permute-start(f32[64,512]{1,0:T(8,128)S(1)} %pad_maximum_fusion.3), channel_id=1, source_target_pairs={{0,0},{1,32},{2,64},{3,96},{4,128},{5,160},{6,192},{7,224},{8,1},{... | collective-permute-start | bytes 393224 | tf_op jit(solution)/shard_map/ppermute | solution.py:58
  20.7 48.5 %all-to-all-start = ((f32[8,64,512]{2,1,0:T(8,128)}), f32[8,64,512]{2,1,0:T(8,128)S(1)}, u32[]{:S(2)}, u32[]{:S(2)}) async-start(f32[8,64,512]{2,1,0:T(8,128)} %tile.12), calls=%async_computation | async-start | bytes 2097152 | tf_op jit(solution)/shard_map/all_to_all | solution.py:44
  39.9 224.7 %all-gather.6.cloned.1.call-start = ((), (), s32[]{:S(2)}) async-start(), calls=%async_computation.10 | async-start | bytes 4325376 | tf_op jit(solution)/shard_map/all_gather | solution.py:93
  80.4 11.8 %collective-permute-start.7 = (f32[64,512]{0,1:T(8,128)S(1)}, f32[64,512]{0,1:T(8,128)S(1)}, u32[]{:S(2)}, u32[]{:S(2)}) collective-permute-start(f32[64,512]{0,1:T(8,128)S(1)} %get-tuple-element.24), channel_id=1, source_target_pairs={{0,224},{1,225},{2,226},{3,227},{4,228},{5,229},{6,230},{7,231},{8... | collective-permute-start | bytes 393224 | tf_op jit(solution)/shard_map/ppermute | solution.py:69
  84.3 11.0 %collective-permute-start.6 = (f32[64,512]{0,1:T(8,128)S(1)}, f32[64,512]{0,1:T(8,128)S(1)}, u32[]{:S(2)}, u32[]{:S(2)}) collective-permute-start(f32[64,512]{0,1:T(8,128)S(1)} %get-tuple-element.25), channel_id=1, source_target_pairs={{0,192},{1,193},{2,194},{3,195},{4,196},{5,197},{6,198},{7,199},{8... | collective-permute-start | bytes 393224 | tf_op jit(solution)/shard_map/ppermute | solution.py:69
  85.8 15.3 %collective-permute-start.5 = (f32[64,512]{0,1:T(8,128)}, f32[64,512]{0,1:T(8,128)}, u32[]{:S(2)}, u32[]{:S(2)}) collective-permute-start(f32[64,512]{0,1:T(8,128)} %get-tuple-element.26), channel_id=1, source_target_pairs={{0,160},{1,161},{2,162},{3,163},{4,164},{5,165},{6,166},{7,167},{8... | collective-permute-start | bytes 393224 | tf_op jit(solution)/shard_map/ppermute | solution.py:69
  88.0 13.1 %collective-permute-start.4 = (f32[64,512]{0,1:T(8,128)S(1)}, f32[64,512]{0,1:T(8,128)}, u32[]{:S(2)}, u32[]{:S(2)}) collective-permute-start(f32[64,512]{0,1:T(8,128)S(1)} %get-tuple-element.27), channel_id=1, source_target_pairs={{0,128},{1,129},{2,130},{3,131},{4,132},{5,133},{6,134},{7,135},{8... | collective-permute-start | bytes 393224 | tf_op jit(solution)/shard_map/ppermute | solution.py:69
  90.2 10.9 %collective-permute-start.3 = (f32[64,512]{0,1:T(8,128)S(1)}, f32[64,512]{0,1:T(8,128)}, u32[]{:S(2)}, u32[]{:S(2)}) collective-permute-start(f32[64,512]{0,1:T(8,128)S(1)} %get-tuple-element.28), channel_id=1, source_target_pairs={{0,96},{1,97},{2,98},{3,99},{4,100},{5,101},{6,102},{7,103},{8,104... | collective-permute-start | bytes 393224 | tf_op jit(solution)/shard_map/ppermute | solution.py:69
  92.2 13.9 %collective-permute-start.2 = (f32[64,512]{0,1:T(8,128)S(1)}, f32[64,512]{0,1:T(8,128)}, u32[]{:S(2)}, u32[]{:S(2)}) collective-permute-start(f32[64,512]{0,1:T(8,128)S(1)} %get-tuple-element.29), channel_id=1, source_target_pairs={{0,64},{1,65},{2,66},{3,67},{4,68},{5,69},{6,70},{7,71},{8,72},{9,... | collective-permute-start | bytes 393224 | tf_op jit(solution)/shard_map/ppermute | solution.py:69
  96.1 15.7 %collective-permute-start.1 = (f32[64,512]{0,1:T(8,128)S(1)}, f32[64,512]{0,1:T(8,128)}, u32[]{:S(2)}, u32[]{:S(2)}) collective-permute-start(f32[64,512]{0,1:T(8,128)S(1)} %get-tuple-element.23), channel_id=1, source_target_pairs={{0,32},{1,33},{2,34},{3,35},{4,36},{5,37},{6,38},{7,39},{8,40},{9,... | collective-permute-start | bytes 393224 | tf_op jit(solution)/shard_map/ppermute | solution.py:69
  113.3 25.5 %collective-permute-start.8 = (f32[64,512]{0,1:T(8,128)S(1)}, f32[64,512]{0,1:T(8,128)S(1)}, u32[]{:S(2)}, u32[]{:S(2)}) collective-permute-start(f32[64,512]{0,1:T(8,128)S(1)} %fusion.38), channel_id=1, source_target_pairs={{0,0},{32,1},{64,2},{96,3},{128,4},{160,5},{192,6},{224,7},{1,8},{... | collective-permute-start | bytes 393224 | tf_op jit(solution)/shard_map/ppermute | solution.py:62
  182.7 18.8 %all-to-all-start.5 = ((f32[32,8,768]{2,1,0:T(8,128)}), f32[32,8,768]{2,1,0:T(8,128)S(1)}, u32[]{:S(2)}, u32[]{:S(2)}) async-start(f32[32,8,768]{2,1,0:T(8,128)} %tile.15), calls=%async_computation.5 | async-start | bytes 1572864 | tf_op jit(solution)/shard_map/all_to_all | solution.py:44
  201.5 60.3 %copy-start.5 = (f32[32,8,768]{2,1,0:T(8,128)}, f32[32,8,768]{2,1,0:T(8,128)S(1)}, u32[]{:S(2)}) copy-start(f32[32,8,768]{2,1,0:T(8,128)S(1)} %all-to-all-done.5) | copy-start | bytes 2359300
  271.8 22.6 %all-to-all-start.1 = ((f32[8,64,256]{2,1,0:T(8,128)}), f32[8,64,256]{2,1,0:T(8,128)S(1)}, u32[]{:S(2)}, u32[]{:S(2)}) async-start(f32[8,64,256]{2,1,0:T(8,128)} %bitcast.3), calls=%async_computation.1 | async-start | bytes 1048576 | tf_op jit(solution)/shard_map/all_to_all | solution.py:53
  295.7 16.7 %all-to-all-start.6 = ((f32[32,8,512]{2,1,0:T(8,128)}), f32[32,8,512]{2,1,0:T(8,128)S(1)}, u32[]{:S(2)}, u32[]{:S(2)}) async-start(f32[32,8,512]{2,1,0:T(8,128)} %maximum_bitcast_fusion.2), calls=%async_computation.6 | async-start | bytes 1048576 | tf_op jit(solution)/shard_map/all_to_all | solution.py:53
  313.1 13.1 %all-to-all-start.7 = ((f32[8,8,512]{2,1,0:T(8,128)}), f32[8,8,512]{2,1,0:T(8,128)S(1)}, u32[]{:S(2)}, u32[]{:S(2)}) async-start(f32[8,8,512]{2,1,0:T(8,128)} %tile.16), calls=%async_computation.7 | async-start | bytes 262144 | tf_op jit(solution)/shard_map/all_to_all | solution.py:44
  327.1 15.7 %all-to-all-start.8 = ((f32[32,8,512]{2,1,0:T(8,128)}), f32[32,8,512]{2,1,0:T(8,128)S(1)}, u32[]{:S(2)}, u32[]{:S(2)}) async-start(f32[32,8,512]{2,1,0:T(8,128)} %tile.17), calls=%async_computation.8 | async-start | bytes 1048576 | tf_op jit(solution)/shard_map/all_to_all | solution.py:44
  331.0 58.9 %all-gather.8.cloned.1.call-start = ((), (), s32[]{:S(2)}) async-start(), calls=%async_computation.11 | async-start | bytes 1769472 | tf_op jit(solution)/shard_map/all_gather | solution.py:102
  331.5 7.4 %collective-permute-start.9 = (f32[64,256]{1,0:T(8,128)S(1)}, f32[64,256]{1,0:T(8,128)S(1)}, u32[]{:S(2)}, u32[]{:S(2)}) collective-permute-start(f32[64,256]{1,0:T(8,128)S(1)} %reduce_sum.36), channel_id=1, source_target_pairs={{0,0},{32,1},{64,2},{96,3},{128,4},{160,5},{192,6},{224,7},{1,8},{... | collective-permute-start | bytes 196616 | tf_op jit(solution)/shard_map/ppermute | solution.py:62
  344.4 40.2 %all-to-all-start.2 = ((f32[32,64,256]{2,1,0:T(8,128)}), f32[32,64,256]{2,1,0:T(8,128)}, u32[]{:S(2)}, u32[]{:S(2)}) async-start(f32[32,64,256]{2,1,0:T(8,128)} %stack.2), calls=%async_computation.2 | async-start | bytes 4194304 | tf_op jit(solution)/shard_map/all_to_all | solution.py:15
  389.9 5.2 %copy-start.4 = (f32[2048,256]{0,1:T(8,128)S(1)}, f32[2048,256]{0,1:T(8,128)}, u32[]{:S(2)}) copy-start(f32[2048,256]{0,1:T(8,128)} %fusion.7) | copy-start | bytes 6291460
  (9 other events, 22.8 us)
Sparse Core Ops, SparseCore 0:
  10.6 57.5 all-gather.3
  139.8 54.1 all-gather.5
  336.2 35.3 all-gather.7
